TPU v7x, 32 devices: a whole 2x2x4 slice. The times are simulated.
32 devices in a mesh: groups: 2 (over y), seq: 4 (over z), head: 2 (over x), tile: 2 (over core).
Axes of the slice: x: 2, y: 2, z: 4, core: 2. Of those that a mesh axis runs over, the one named last changes fastest.
Arguments:
- query_states: bfloat16 [4608, 3072], P(('groups', 'seq', 'tile'), 'head'), parts along dimension 0, may hold values from -5 to 5
- key_states: bfloat16 [4608, 3072], P(('groups', 'seq', 'tile'), 'head'), parts along dimension 0, may hold values from -5 to 5
- value_states: bfloat16 [4608, 3072], P(('groups', 'seq', 'tile'), 'head'), parts along dimension 0, may hold values from -6 to 6
- residual: bfloat16 [4608, 3072], P(('groups', 'seq', 'tile'), 'head'), parts along dimension 0, may hold values from -6 to 6
- out_weight: bfloat16 [3072, 3072], P(None, 'head'), may hold values from -0.109375 to 0.109375
- gate_scale: float32 [6144], P(('groups', 'head')), parts along dimension 0, may hold values from 2 to 8
Outputs:
- block_out: bfloat16 [4608, 3072], P(('groups', 'seq', 'tile'), 'head'), parts along dimension 0
There are 2 independent parts, one for each index of `groups`. A program takes and returns all parts, laid end to end along the dimension named above; an argument that names none is the same for every part. Nothing has to cross between parts.
All inputs are finite; a program needn't handle non-finite values.
Results may differ from a plain program's by a relative error of at most 0.0065.
Values may be sent and summed in bfloat16 or wider, within the bound.
A program may use at most 128 MiB of HBM per device.

v0:
```python
import math
import jax
import jax.numpy as jnp
from jax import lax
from jax.sharding import PartitionSpec as P

HD = 128


def per_device(query_states, key_states, value_states, residual, out_weight, gate_scale):
    row_count = query_states.shape[0]
    heads_here = query_states.shape[1] // HD
    score_scale = 1.0 / math.sqrt(HD)
    query_heads = query_states.reshape(row_count, heads_here, HD)
    running_max = jnp.full((heads_here, row_count), -jnp.inf, jnp.float32)
    denominator = jnp.zeros((heads_here, row_count), jnp.float32)
    numerator = jnp.zeros((row_count, heads_here, HD), jnp.float32)
    key_heads = lax.all_gather(key_states, ("seq", "tile"), axis=0, tiled=True).reshape(
        -1, heads_here, HD
    )
    value_heads = lax.all_gather(value_states, ("seq", "tile"), axis=0, tiled=True).reshape(
        -1, heads_here, HD
    )
    scores = (
        jnp.einsum("qhd,khd->hqk", query_heads, key_heads, preferred_element_type=jnp.float32)
        * score_scale
    )
    new_max = jnp.max(scores, axis=2)
    shrink = jnp.exp(running_max - new_max)
    weights = jnp.exp(scores - new_max[:, :, None])
    denominator = denominator * shrink + jnp.sum(weights, axis=2)
    probs = weights.astype(jnp.bfloat16)
    numerator = numerator * shrink.T[:, :, None] + jnp.einsum(
        "hqk,khd->qhd", probs, value_heads, preferred_element_type=jnp.float32
    )
    running_max, denominator, numerator = (new_max, denominator, numerator)
    attended = (
        (numerator / denominator.T[:, :, None])
        .astype(jnp.bfloat16)
        .reshape(row_count, heads_here * HD)
    )
    projected = jnp.dot(
        lax.all_gather(attended, "head", axis=1, tiled=True),
        out_weight,
        preferred_element_type=jnp.float32,
    )
    return (residual.astype(jnp.float32) + gate_scale[None, :] * projected).astype(jnp.bfloat16)


def solution(mesh):
    placed = (
        P(("groups", "seq", "tile"), "head"),
        P(("groups", "seq", "tile"), "head"),
        P(("groups", "seq", "tile"), "head"),
        P(("groups", "seq", "tile"), "head"),
        P(None, "head"),
        P(("groups", "head")),
    )
    return jax.shard_map(
        per_device,
        mesh=mesh,
        in_specs=placed,
        out_specs=P(("groups", "seq", "tile"), "head"),
        check_vma=False,
    )
```

profile of v0, /device:TPU:0, one launch (start us, length us, event | category | flops | bytes accessed | tf_op | source)
XLA Modules:
  0.0 223.8 jit_solution(13114338873008730694)
XLA Ops:
  6.5 0.0 copy-start
  6.5 0.0 all-gather.4.cloned.1.call-start
  6.5 0.7 all-gather.4.cloned.1.call-update
  7.3 0.0 all-gather.6.cloned.1.call-start
  7.3 0.7 all-gather.6.cloned.1.call-update
  8.0 0.0 all-gather.8.cloned.1.call-start
  8.1 74.9 %all-gather.4.cloned.1.call-done = bf16[2304,1536]{1,0:T(8,128)(2,1)} async-done(((bf16[288,1536]{1,0:T(8,128)(2,1)}), bf16[2304,1536]{1,0:T(8,128)(2,1)}) %all-gather.4.cloned.1.call-update) | async-done | bytes 7077904 | tf_op jit(solution)/shard_map/all_gather | solution.py:18
  83.0 10.3 %copy.14 = bf16[2304,1536]{0,1:T(8,128)(2,1)} copy(bf16[2304,1536]{1,0:T(8,128)(2,1)} %all-gather.4.cloned.1.call-done) | data formatting | bytes 14155776 | tf_op jit(solution)/shard_map/all_gather | solution.py:18
  93.3 0.0 copy-done
  93.3 14.8 %multiply_reduce_fusion = (f32[12,288]{1,0:T(8,128)S(1)}, f32[12,288,2304]{2,1,0:T(8,128)}) fusion(bf16[2304,12,128]{0,2,1:T(8,128)(2,1)} %bitcast.34, bf16[288,1536]{1,0:T(8,128)(2,1)S(1)} %copy-done), kind=kOutput, calls=%fused_computation.1 | convolution fusion | flops 2054353536 | bytes 39826944 | tf_op jit(solution)/shard_map/qhd,khd->hqk/dot_general | solution.py:25
  108.2 14.0 %fusion = f32[12,288]{1,0:T(8,128)S(1)} fusion(f32[12,288,2304]{2,1,0:T(8,128)} %get-tuple-element.6, f32[12,288]{1,0:T(8,128)S(1)} %get-tuple-element.5), kind=kLoop, calls=%fused_computation.2 | loop fusion | flops 23884416 | bytes 31878144 | tf_op jit(solution)/shard_map/reduce_sum | solution.py:31
  122.2 32.4 %all-gather.6.cloned.1.call-done = bf16[2304,1536]{1,0:T(8,128)(2,1)} async-done(((bf16[288,1536]{1,0:T(8,128)(2,1)}), bf16[2304,1536]{1,0:T(8,128)(2,1)}) %all-gather.6.cloned.1.call-update) | async-done | bytes 7077904 | tf_op jit(solution)/shard_map/all_gather | solution.py:21
  154.5 10.3 %copy.17 = bf16[2304,1536]{0,1:T(8,128)(2,1)} copy(bf16[2304,1536]{1,0:T(8,128)(2,1)} %all-gather.6.cloned.1.call-done) | data formatting | bytes 14155776 | tf_op jit(solution)/shard_map/all_gather | solution.py:21
  164.8 0.0 copy-start.2
  164.8 0.0 copy-start.3
  164.8 15.1 %fusion.12 = bf16[12,36,8,128]{3,2,1,0:T(8,128)(2,1)S(1)} fusion(bf16[2304,12,128]{0,2,1:T(8,128)(2,1)} %bitcast.35, f32[12,288,2304]{2,1,0:T(8,128)} %get-tuple-element.6, f32[12,288]{1,0:T(8,128)S(1)} %get-tuple-element.5, f32[288,12]{0,1:T(8,128)S(1)} %bitcast_add_fusion.1, f32[288,12]{0,1:T(8,128)S(1)} %multiply_bitcast_fusion), kind=kOutput, calls=%fused_computation.13 | convolution fusion | flops 2063646720 | bytes 39854592 | tf_op jit(solution)/shard_map/hqk,khd->qhd/dot_general | solution.py:33
  179.9 1.1 copy.31
  181.0 0.0 all-gather.8.cloned.1.call-update
  181.0 28.2 %all-gather.8.cloned.1.call-done = bf16[288,3072]{1,0:T(8,128)(2,1)} async-done(((bf16[288,1536]{1,0:T(8,128)(2,1)}), bf16[288,3072]{1,0:T(8,128)(2,1)}) %all-gather.8.cloned.1.call-update) | async-done | bytes 1769488 | tf_op jit(solution)/shard_map/all_gather | solution.py:43
  209.2 0.0 copy-done.2
  209.2 0.0 copy-done.3
  209.2 0.0 copy-start.1
  209.2 8.1 %fusion.7 = bf16[288,1536]{1,0:T(8,128)(2,1)} fusion(bf16[288,3072]{1,0:T(8,128)(2,1)} %all-gather.8.cloned.1.call-done, bf16[3072,1536]{1,0:T(8,128)(2,1)} %param.10, bf16[288,1536]{1,0:T(8,128)(2,1)S(1)} %copy-done.2, f32[1536]{0:T(1024)S(1)} %copy-done.3), kind=kOutput, calls=%fused_computation.9 | convolution fusion | flops 2719678464 | bytes 12982272 | tf_op jit(solution)/shard_map/dot_general | solution.py:42
  217.3 0.0 copy-done.1
  (2 shorter events, 0.0 us)
Async XLA Ops:
  6.5 86.8 %copy-start = (bf16[288,1536]{1,0:T(8,128)(2,1)S(1)}, bf16[288,1536]{1,0:T(8,128)(2,1)}, u32[]{:S(2)}) copy-start(bf16[288,1536]{1,0:T(8,128)(2,1)} %param.6) | copy-start | bytes 2654212
  6.5 76.5 %all-gather.4.cloned.1.call-start = ((), (), s32[]{:S(2)}) async-start(), calls=%async_computation | async-start | bytes 7962624 | tf_op jit(solution)/shard_map/all_gather | solution.py:18
  7.3 147.3 %all-gather.6.cloned.1.call-start = ((), (), s32[]{:S(2)}) async-start(), calls=%async_computation.1 | async-start | bytes 7962624 | tf_op jit(solution)/shard_map/all_gather | solution.py:21
  8.0 201.2 %all-gather.8.cloned.1.call-start = ((), (), s32[]{:S(2)}) async-start(), calls=%async_computation.2 | async-start | bytes 2654208 | tf_op jit(solution)/shard_map/all_gather | solution.py:43
  164.8 44.4 %copy-start.2 = (bf16[288,1536]{1,0:T(8,128)(2,1)S(1)}, bf16[288,1536]{1,0:T(8,128)(2,1)}, u32[]{:S(2)}) copy-start(bf16[288,1536]{1,0:T(8,128)(2,1)} %param.9) | copy-start | bytes 2654212
  164.8 44.4 %copy-start.3 = (f32[1536]{0:T(1024)S(1)}, f32[1536]{0:T(1024)}, u32[]{:S(2)}) copy-start(f32[1536]{0:T(1024)} %param.11) | copy-start | bytes 18436
  209.2 8.1 %copy-start.1 = (bf16[288,1536]{1,0:T(8,128)(2,1)S(1)}, bf16[288,1536]{1,0:T(8,128)(2,1)}, u32[]{:S(2)}) copy-start(bf16[288,1536]{1,0:T(8,128)(2,1)} %param.6) | copy-start | bytes 2654212
Sparse Core Ops, SparseCore 0:
  9.0 73.9 all-gather.3
  84.6 69.8 all-gather.5
  181.1 28.0 all-gather.7
where the time goes:
time: 225 us; the launch traced here: 224 us
  waiting for transfers between devices  137 us (61%)
  matrix products  38 us (17%)
  local copies, waits for them, and re-layouts  21.7 us (10%)
  other arithmetic  14 us (6%)
  between operations  13.1 us (6%)
    all_gather x1, waiting for transfers between devices, per_device(): lax.all_gather(key_states, ('seq', 'tile'), axis=0, tiled=True)  74.9 us
    all_gather x1, waiting for transfers between devices, per_device(): lax.all_gather(value_states, ('seq', 'tile'), axis=0, tiled=True)  32.4 us
    all_gather x1, waiting for transfers between devices, per_device(): lax.all_gather(attended, 'head', axis=1, tiled=True)  28.2 us
    dot_general x1, matrix products, per_device(): jnp.einsum('hqk,khd->qhd', probs, value_heads, preferred_element_type=jnp...  15.1 us
    dot_general x1, matrix products, per_device(): jnp.einsum('qhd,khd->hqk', query_heads, key_heads, preferred_element_type...  14.8 us
    reduce_sum x1, other arithmetic, per_device(): denominator = denominator * shrink + jnp.sum(weights, axis=2)  14 us
    all_gather x1, local copies, waits for them, and re-layouts, per_device(): lax.all_gather(key_states, ('seq', 'tile'), axis=0, tiled=True)  10.3 us
    all_gather x1, local copies, waits for them, and re-layouts, per_device(): lax.all_gather(value_states, ('seq', 'tile'), axis=0, tiled=True)  10.3 us
  transfers between devices with their start and end apart: 3, of which 3 were waited for; matrix products, arithmetic and copies ran while one was open for 17% of the time, Pallas kernels for 0%

commit v1 on v0

--- a/solution.py
+++ b/solution.py
@@ -5,6 +5,27 @@
 from jax.sharding import PartitionSpec as P
 
 HD = 128
+
+
+def gather_around(array, axis, dim):
+    size, position, rows = (lax.axis_size(axis), lax.axis_index(axis), array.shape[dim])
+    right = [(i, (i + 1) % size) for i in range(size)]
+    behind = [(i, (i - 1) % size) for i in range(size)]
+    out = jnp.zeros((*array.shape[:dim], size * rows, *array.shape[dim + 1 :]), array.dtype)
+    out = lax.dynamic_update_slice_in_dim(out, array, position * rows, axis=dim)
+    from_left = from_right = array
+    half = size // 2
+    for step in range(1, half + 1):
+        from_left = lax.ppermute(from_left, axis, right)
+        out = lax.dynamic_update_slice_in_dim(
+            out, from_left, (position - step) % size * rows, axis=dim
+        )
+        if step < size - half:
+            from_right = lax.ppermute(from_right, axis, behind)
+            out = lax.dynamic_update_slice_in_dim(
+                out, from_right, (position + step) % size * rows, axis=dim
+            )
+    return out
 
 
 def per_device(query_states, key_states, value_states, residual, out_weight, gate_scale):
@@ -15,9 +36,7 @@
     running_max = jnp.full((heads_here, row_count), -jnp.inf, jnp.float32)
     denominator = jnp.zeros((heads_here, row_count), jnp.float32)
     numerator = jnp.zeros((row_count, heads_here, HD), jnp.float32)
-    key_heads = lax.all_gather(key_states, ("seq", "tile"), axis=0, tiled=True).reshape(
-        -1, heads_here, HD
-    )
+    key_heads = gather_around(key_states, ("seq", "tile"), 0).reshape(-1, heads_here, HD)
     value_heads = lax.all_gather(value_states, ("seq", "tile"), axis=0, tiled=True).reshape(
         -1, heads_here, HD
     )

time: 225 us -> 345 us (1.53)
  local copies, waits for them, and re-layouts: 21.7 us -> 124 us
  starting transfers between devices: 0.08 us -> 21.5 us
  waiting for transfers between devices: 137 us -> 131 us
    dynamic_update_slice x0 -> x8, local copies, waits for them, and re-layouts: none -> 97.3 us  [the longest x4 48.2 us: gather_around(): lax.dynamic_update_slice_in_dim(out, from_left, (position - step) % size...]
    ppermute x0 -> x7, waiting for transfers between devices: none -> 88.8 us  [the longest x4 71.2 us: gather_around(): from_left = lax.ppermute(from_left, axis, right)]
    all_gather x1 -> x0, waiting for transfers between devices: 74.9 us -> none  [per_device(): lax.all_gather(key_states, ('seq', 'tile'), axis=0, tiled=True)]
    all_gather x1, waiting for transfers between devices: 32.4 us -> 0.02 us  [per_device(): lax.all_gather(value_states, ('seq', 'tile'), axis=0, tiled=True)]
    ppermute x0 -> x7, starting transfers between devices: none -> 21.5 us  [the longest x3 11.6 us: gather_around(): from_right = lax.ppermute(from_right, axis, behind)]
    all_gather x1, waiting for transfers between devices: 28.2 us -> 41.2 us  [per_device(): lax.all_gather(attended, 'head', axis=1, tiled=True)]
    ppermute x0 -> x7, local copies, waits for them, and re-layouts: none -> 10.6 us  [the longest x4 5.65 us: gather_around(): from_left = lax.ppermute(from_left, axis, right)]
    all_gather x1 -> x0, local copies, waits for them, and re-layouts: 10.3 us -> none  [per_device(): lax.all_gather(key_states, ('seq', 'tile'), axis=0, tiled=True)]
  transfers between devices with their start and end apart: 3 -> 9, of which waited for: 3 -> 6; matrix products, arithmetic and copies ran while one was open for 17% -> 41% of each run, Pallas kernels for 0% -> 0%
where the time goes in v1:
time: 345 us; the launch traced here: 342 us
  waiting for transfers between devices  131 us (38%)
  local copies, waits for them, and re-layouts  124 us (36%)
  matrix products  37.8 us (11%)
  starting transfers between devices  21.5 us (6%)
  other arithmetic  13.9 us (4%)
  between operations  13.6 us (4%)
    ppermute x4, waiting for transfers between devices, gather_around(): from_left = lax.ppermute(from_left, axis, right)  71.2 us
    dynamic_update_slice x4, local copies, waits for them, and re-layouts, gather_around(): lax.dynamic_update_slice_in_dim(out, from_left, (position - step) % size...  48.2 us
    all_gather x1, waiting for transfers between devices, per_device(): lax.all_gather(attended, 'head', axis=1, tiled=True)  41.2 us
    dynamic_update_slice x3, local copies, waits for them, and re-layouts, gather_around(): lax.dynamic_update_slice_in_dim(out, from_right, (position + step) % size...  37.8 us
    ppermute x3, waiting for transfers between devices, gather_around(): from_right = lax.ppermute(from_right, axis, behind)  17.6 us
    dot_general x1, matrix products, per_device(): jnp.einsum('hqk,khd->qhd', probs, value_heads, preferred_element_type=jnp...  15.1 us
    dot_general x1, matrix products, per_device(): jnp.einsum('qhd,khd->hqk', query_heads, key_heads, preferred_element_type...  14.6 us
    reduce_sum x1, other arithmetic, per_device(): denominator = denominator * shrink + jnp.sum(weights, axis=2)  13.8 us
  transfers between devices with their start and end apart: 9, of which 6 were waited for; matrix products, arithmetic and copies ran while one was open for 41% of the time, Pallas kernels for 0%

profile of v1, /device:TPU:0, one launch (start us, length us, event | category | flops | bytes accessed | tf_op | source)
XLA Modules:
  0.0 341.5 jit_solution(5106186980798070295)
XLA Ops:
  6.5 0.0 copy-start
  6.5 0.0 all-gather.3.cloned.1.call-start
  6.5 0.7 all-gather.3.cloned.1.call-update
  7.3 0.0 all-gather.5.cloned.1.call-start
  7.3 0.5 collective-permute-start
  7.8 4.1 %collective-permute-start.1 = (bf16[288,1536]{1,0:T(8,128)(2,1)}, bf16[288,1536]{1,0:T(8,128)(2,1)S(1)}, u32[]{:S(2)}, u32[]{:S(2)}) collective-permute-start(bf16[288,1536]{1,0:T(8,128)(2,1)} %param.7), channel_id=1, source_target_pairs={{0,13},{1,0},{4,1},{5,4},{8,5},{9,8},{12,9},{13,12},{2,15},{3,2},{... | collective-permute-start | bytes 2654216 | tf_op jit(solution)/shard_map/ppermute | solution.py:24
  11.9 22.8 %collective-permute-done = bf16[288,1536]{1,0:T(8,128)(2,1)S(1)} collective-permute-done((bf16[288,1536]{1,0:T(8,128)(2,1)}, bf16[288,1536]{1,0:T(8,128)(2,1)S(1)}, u32[]{:S(2)}, u32[]{:S(2)}) %collective-permute-start) | collective-permute-done | bytes 884768 | tf_op jit(solution)/shard_map/ppermute | solution.py:19
  34.7 0.0 copy-start.4
  34.7 0.8 collective-permute-start.2
  35.5 7.6 %collective-permute-done.1 = bf16[288,1536]{1,0:T(8,128)(2,1)S(1)} collective-permute-done((bf16[288,1536]{1,0:T(8,128)(2,1)}, bf16[288,1536]{1,0:T(8,128)(2,1)S(1)}, u32[]{:S(2)}, u32[]{:S(2)}) %collective-permute-start.1) | collective-permute-done | bytes 884768 | tf_op jit(solution)/shard_map/ppermute | solution.py:24
  43.1 0.0 copy-start.2
  43.1 3.6 %collective-permute-start.3 = (bf16[288,1536]{1,0:T(8,128)(2,1)S(1)}, bf16[288,1536]{1,0:T(8,128)(2,1)}, u32[]{:S(2)}, u32[]{:S(2)}) collective-permute-start(bf16[288,1536]{1,0:T(8,128)(2,1)S(1)} %collective-permute-done.1), channel_id=1, source_target_pairs={{0,13},{1,0},{4,1},{5,4},{8,5},{9,8},{12,9},{13,12},{2,15},{3,2},{... | collective-permute-start | bytes 2654216 | tf_op jit(solution)/shard_map/ppermute | solution.py:24
  46.7 26.9 %collective-permute-done.2 = bf16[288,1536]{1,0:T(8,128)(2,1)S(1)} collective-permute-done((bf16[288,1536]{1,0:T(8,128)(2,1)S(1)}, bf16[288,1536]{1,0:T(8,128)(2,1)S(1)}, u32[]{:S(2)}, u32[]{:S(2)}) %collective-permute-start.2) | collective-permute-done | bytes 884768 | tf_op jit(solution)/shard_map/ppermute | solution.py:19
  73.6 0.0 copy-start.3
  73.6 1.0 collective-permute-start.4
  74.7 10.0 %collective-permute-done.3 = bf16[288,1536]{1,0:T(8,128)(2,1)} collective-permute-done((bf16[288,1536]{1,0:T(8,128)(2,1)S(1)}, bf16[288,1536]{1,0:T(8,128)(2,1)}, u32[]{:S(2)}, u32[]{:S(2)}) %collective-permute-start.3) | collective-permute-done | bytes 884768 | tf_op jit(solution)/shard_map/ppermute | solution.py:24
  84.7 3.8 %collective-permute-start.5 = (bf16[288,1536]{1,0:T(8,128)(2,1)}, bf16[288,1536]{1,0:T(8,128)(2,1)}, u32[]{:S(2)}, u32[]{:S(2)}) collective-permute-start(bf16[288,1536]{1,0:T(8,128)(2,1)} %collective-permute-done.3), channel_id=1, source_target_pairs={{0,13},{1,0},{4,1},{5,4},{8,5},{9,8},{12,9},{13,12},{2,15},{3,2},{... | collective-permute-start | bytes 2654216 | tf_op jit(solution)/shard_map/ppermute | solution.py:24
  88.5 21.5 %collective-permute-done.4 = bf16[288,1536]{1,0:T(8,128)(2,1)S(1)} collective-permute-done((bf16[288,1536]{1,0:T(8,128)(2,1)S(1)}, bf16[288,1536]{1,0:T(8,128)(2,1)S(1)}, u32[]{:S(2)}, u32[]{:S(2)}) %collective-permute-start.4) | collective-permute-done | bytes 884768 | tf_op jit(solution)/shard_map/ppermute | solution.py:19
  110.0 0.0 copy-done.2
  110.0 7.5 %collective-permute-start.6 = (bf16[288,1536]{1,0:T(8,128)(2,1)S(1)}, bf16[288,1536]{1,0:T(8,128)(2,1)}, u32[]{:S(2)}, u32[]{:S(2)}) collective-permute-start(bf16[288,1536]{1,0:T(8,128)(2,1)S(1)} %collective-permute-done.4), channel_id=1, source_target_pairs={{0,1},{1,4},{4,5},{5,8},{8,9},{9,12},{12,13},{13,0},{2,3},{3,6},{6... | collective-permute-start | bytes 2654216 | tf_op jit(solution)/shard_map/ppermute | solution.py:19
  117.6 0.0 copy-done.4
  117.6 0.0 copy-done.3
  117.6 1.6 copy.16
  119.3 3.3 broadcast_in_dim.7
  122.5 11.3 %dynamic_update_slice.24 = bf16[2304,1536]{0,1:T(8,128)(2,1)} dynamic-update-slice(bf16[2304,1536]{0,1:T(8,128)(2,1)} %broadcast_in_dim.7, bf16[288,1536]{0,1:T(8,128)(2,1)S(1)} %copy.16, s32[]{:T(128)S(6)} %select_n.55, s32[]{:T(128)} %constant.65.clone.1) | dynamic-update-slice | bytes 1769476 | tf_op jit(solution)/shard_map/dynamic_update_slice | solution.py:15
  133.8 1.6 copy.17
  135.5 11.8 %dynamic_update_slice.25 = bf16[2304,1536]{0,1:T(8,128)(2,1)} dynamic-update-slice(bf16[2304,1536]{0,1:T(8,128)(2,1)} %dynamic_update_slice.24, bf16[288,1536]{0,1:T(8,128)(2,1)S(1)} %copy.17, s32[]{:T(128)S(6)} %select_n.57, s32[]{:T(128)} %constant.65.clone.1) | dynamic-update-slice | bytes 1769476 | tf_op jit(solution)/shard_map/dynamic_update_slice | solution.py:20
  147.3 1.6 copy.18
  149.0 12.6 %dynamic_update_slice.26 = bf16[2304,1536]{0,1:T(8,128)(2,1)} dynamic-update-slice(bf16[2304,1536]{0,1:T(8,128)(2,1)} %dynamic_update_slice.25, bf16[288,1536]{0,1:T(8,128)(2,1)S(1)} %copy.18, s32[]{:T(128)S(6)} %select_n.59, s32[]{:T(128)} %constant.65.clone.1) | dynamic-update-slice | bytes 1769476 | tf_op jit(solution)/shard_map/dynamic_update_slice | solution.py:25
  161.6 1.6 copy.19
  163.2 12.4 %dynamic_update_slice.27 = bf16[2304,1536]{0,1:T(8,128)(2,1)} dynamic-update-slice(bf16[2304,1536]{0,1:T(8,128)(2,1)} %dynamic_update_slice.26, bf16[288,1536]{0,1:T(8,128)(2,1)S(1)} %copy.19, s32[]{:T(128)S(6)} %select_n.61, s32[]{:T(128)} %constant.65.clone.1) | dynamic-update-slice | bytes 1769476 | tf_op jit(solution)/shard_map/dynamic_update_slice | solution.py:20
  175.7 1.6 copy.20
  177.3 12.6 %dynamic_update_slice.28 = bf16[2304,1536]{0,1:T(8,128)(2,1)} dynamic-update-slice(bf16[2304,1536]{0,1:T(8,128)(2,1)} %dynamic_update_slice.27, bf16[288,1536]{0,1:T(8,128)(2,1)S(1)} %copy.20, s32[]{:T(128)S(6)} %select_n.63, s32[]{:T(128)} %constant.65.clone.1) | dynamic-update-slice | bytes 1769476 | tf_op jit(solution)/shard_map/dynamic_update_slice | solution.py:25
  189.9 0.7 copy.21
  190.6 12.6 %dynamic_update_slice.29 = bf16[2304,1536]{0,1:T(8,128)(2,1)} dynamic-update-slice(bf16[2304,1536]{0,1:T(8,128)(2,1)} %dynamic_update_slice.28, bf16[288,1536]{0,1:T(8,128)(2,1)S(1)} %copy.21, s32[]{:T(128)S(6)} %select_n.65, s32[]{:T(128)} %constant.65.clone.1) | dynamic-update-slice | bytes 1769476 | tf_op jit(solution)/shard_map/dynamic_update_slice | solution.py:20
  203.2 0.0 collective-permute-done.5
  203.2 1.6 copy.22
  204.9 12.6 %dynamic_update_slice.30 = bf16[2304,1536]{0,1:T(8,128)(2,1)} dynamic-update-slice(bf16[2304,1536]{0,1:T(8,128)(2,1)} %dynamic_update_slice.29, bf16[288,1536]{0,1:T(8,128)(2,1)S(1)} %copy.22, s32[]{:T(128)S(6)} %select_n.67, s32[]{:T(128)} %constant.65.clone.1) | dynamic-update-slice | bytes 1769476 | tf_op jit(solution)/shard_map/dynamic_update_slice | solution.py:25
  217.5 0.0 collective-permute-done.6
  217.5 1.6 copy.23
  219.1 11.3 %dynamic_update_slice.31 = bf16[2304,1536]{0,1:T(8,128)(2,1)} dynamic-update-slice(bf16[2304,1536]{0,1:T(8,128)(2,1)} %dynamic_update_slice.30, bf16[288,1536]{0,1:T(8,128)(2,1)S(1)} %copy.23, s32[]{:T(128)S(6)} %select_n.69, s32[]{:T(128)} %constant.65.clone.1) | dynamic-update-slice | bytes 1769476 | tf_op jit(solution)/shard_map/dynamic_update_slice | solution.py:20
  230.5 0.0 copy-done
  230.5 14.6 %bitcast_reduce_fusion = (f32[12,288]{1,0:T(8,128)S(1)}, f32[12,2304,288]{1,2,0:T(8,128)}) fusion(bf16[2304,12,128]{0,2,1:T(8,128)(2,1)} %bitcast.48, bf16[288,1536]{1,0:T(8,128)(2,1)S(1)} %copy-done), kind=kOutput, calls=%fused_computation.1 | convolution fusion | flops 2054353536 | bytes 39826944 | tf_op jit(solution)/shard_map/qhd,khd->hqk/dot_general | solution.py:44
  245.0 13.8 %fusion.1 = f32[12,288]{1,0:T(8,128)S(1)} fusion(f32[12,2304,288]{1,2,0:T(8,128)} %get-tuple-element.6, f32[12,288]{1,0:T(8,128)S(1)} %get-tuple-element.5), kind=kLoop, calls=%fused_computation.3 | loop fusion | flops 23884416 | bytes 31878144 | tf_op jit(solution)/shard_map/reduce_sum | solution.py:50
  258.9 0.0 all-gather.3.cloned.1.call-done
  258.9 10.2 %copy.26 = bf16[2304,1536]{0,1:T(8,128)(2,1)} copy(bf16[2304,1536]{1,0:T(8,128)(2,1)} %all-gather.3.cloned.1.call-done) | data formatting | bytes 14155776 | tf_op jit(solution)/shard_map/all_gather | solution.py:40
  269.2 0.0 copy-start.5
  269.2 0.0 copy-start.6
  269.2 15.1 %fusion.13 = bf16[12,36,8,128]{3,2,1,0:T(8,128)(2,1)S(1)} fusion(bf16[2304,12,128]{0,2,1:T(8,128)(2,1)} %bitcast.49, f32[12,2304,288]{1,2,0:T(8,128)} %get-tuple-element.6, f32[12,288]{1,0:T(8,128)S(1)} %get-tuple-element.5, f32[288,12]{0,1:T(8,128)S(1)} %bitcast_add_fusion.1, f32[288,12]{0,1:T(8,128)S(1)} %multiply_bitcast_fusion), kind=kOutput, calls=%fused_computation.14 | convolution fusion | flops 2063646720 | bytes 39854592 | tf_op jit(solution)/shard_map/hqk,khd->qhd/dot_general | solution.py:52
  284.3 1.1 copy.40
  285.4 0.0 all-gather.5.cloned.1.call-update
  285.4 41.2 %all-gather.5.cloned.1.call-done = bf16[288,3072]{1,0:T(8,128)(2,1)} async-done(((bf16[288,1536]{1,0:T(8,128)(2,1)}), bf16[288,3072]{1,0:T(8,128)(2,1)}) %all-gather.5.cloned.1.call-update) | async-done | bytes 1769488 | tf_op jit(solution)/shard_map/all_gather | solution.py:62
  326.6 0.0 copy-done.5
  326.6 0.0 copy-done.6
  326.6 0.0 copy-start.1
  326.6 8.1 %fusion.8 = bf16[288,1536]{1,0:T(8,128)(2,1)} fusion(bf16[288,3072]{1,0:T(8,128)(2,1)} %all-gather.5.cloned.1.call-done, bf16[3072,1536]{1,0:T(8,128)(2,1)} %param.10, bf16[288,1536]{1,0:T(8,128)(2,1)S(1)} %copy-done.5, f32[1536]{0:T(1024)S(1)} %copy-done.6), kind=kOutput, calls=%fused_computation.10 | convolution fusion | flops 2719678464 | bytes 12982272 | tf_op jit(solution)/shard_map/dot_general | solution.py:61
  334.7 0.0 copy-done.1
  (2 shorter events, 0.0 us)
Async XLA Ops:
  6.5 223.9 %copy-start = (bf16[288,1536]{1,0:T(8,128)(2,1)S(1)}, bf16[288,1536]{1,0:T(8,128)(2,1)}, u32[]{:S(2)}) copy-start(bf16[288,1536]{1,0:T(8,128)(2,1)} %param.6) | copy-start | bytes 2654212
  6.5 252.4 %all-gather.3.cloned.1.call-start = ((), (), s32[]{:S(2)}) async-start(), calls=%async_computation | async-start | bytes 7962624 | tf_op jit(solution)/shard_map/all_gather | solution.py:40
  7.3 319.3 %all-gather.5.cloned.1.call-start = ((), (), s32[]{:S(2)}) async-start(), calls=%async_computation.1 | async-start | bytes 2654208 | tf_op jit(solution)/shard_map/all_gather | solution.py:62
  7.3 27.4 %collective-permute-start = (bf16[288,1536]{1,0:T(8,128)(2,1)}, bf16[288,1536]{1,0:T(8,128)(2,1)S(1)}, u32[]{:S(2)}, u32[]{:S(2)}) collective-permute-start(bf16[288,1536]{1,0:T(8,128)(2,1)} %param.7), channel_id=1, source_target_pairs={{0,1},{1,4},{4,5},{5,8},{8,9},{9,12},{12,13},{13,0},{2,3},{3,6},{6... | collective-permute-start | bytes 2654216 | tf_op jit(solution)/shard_map/ppermute | solution.py:19
  7.8 35.3 %collective-permute-start.1 = (bf16[288,1536]{1,0:T(8,128)(2,1)}, bf16[288,1536]{1,0:T(8,128)(2,1)S(1)}, u32[]{:S(2)}, u32[]{:S(2)}) collective-permute-start(bf16[288,1536]{1,0:T(8,128)(2,1)} %param.7), channel_id=1, source_target_pairs={{0,13},{1,0},{4,1},{5,4},{8,5},{9,8},{12,9},{13,12},{2,15},{3,2},{... | collective-permute-start | bytes 2654216 | tf_op jit(solution)/shard_map/ppermute | solution.py:24
  34.7 82.9 %copy-start.4 = (bf16[288,1536]{1,0:T(8,128)(2,1)}, bf16[288,1536]{1,0:T(8,128)(2,1)S(1)}, u32[]{:S(2)}) copy-start(bf16[288,1536]{1,0:T(8,128)(2,1)S(1)} %collective-permute-done) | copy-start | bytes 2654212
  34.7 38.9 %collective-permute-start.2 = (bf16[288,1536]{1,0:T(8,128)(2,1)S(1)}, bf16[288,1536]{1,0:T(8,128)(2,1)S(1)}, u32[]{:S(2)}, u32[]{:S(2)}) collective-permute-start(bf16[288,1536]{1,0:T(8,128)(2,1)S(1)} %collective-permute-done), channel_id=1, source_target_pairs={{0,1},{1,4},{4,5},{5,8},{8,9},{9,12},{12,13},{13,0},{2,3},{3,6},{6... | collective-permute-start | bytes 2654216 | tf_op jit(solution)/shard_map/ppermute | solution.py:19
  43.1 66.9 %copy-start.2 = (bf16[288,1536]{1,0:T(8,128)(2,1)}, bf16[288,1536]{1,0:T(8,128)(2,1)S(1)}, u32[]{:S(2)}) copy-start(bf16[288,1536]{1,0:T(8,128)(2,1)S(1)} %collective-permute-done.1) | copy-start | bytes 2654212
  43.1 41.6 %collective-permute-start.3 = (bf16[288,1536]{1,0:T(8,128)(2,1)S(1)}, bf16[288,1536]{1,0:T(8,128)(2,1)}, u32[]{:S(2)}, u32[]{:S(2)}) collective-permute-start(bf16[288,1536]{1,0:T(8,128)(2,1)S(1)} %collective-permute-done.1), channel_id=1, source_target_pairs={{0,13},{1,0},{4,1},{5,4},{8,5},{9,8},{12,9},{13,12},{2,15},{3,2},{... | collective-permute-start | bytes 2654216 | tf_op jit(solution)/shard_map/ppermute | solution.py:24
  73.6 44.0 %copy-start.3 = (bf16[288,1536]{1,0:T(8,128)(2,1)}, bf16[288,1536]{1,0:T(8,128)(2,1)S(1)}, u32[]{:S(2)}) copy-start(bf16[288,1536]{1,0:T(8,128)(2,1)S(1)} %collective-permute-done.2) | copy-start | bytes 2654212
  73.6 36.4 %collective-permute-start.4 = (bf16[288,1536]{1,0:T(8,128)(2,1)S(1)}, bf16[288,1536]{1,0:T(8,128)(2,1)S(1)}, u32[]{:S(2)}, u32[]{:S(2)}) collective-permute-start(bf16[288,1536]{1,0:T(8,128)(2,1)S(1)} %collective-permute-done.2), channel_id=1, source_target_pairs={{0,1},{1,4},{4,5},{5,8},{8,9},{9,12},{12,13},{13,0},{2,3},{3,6},{6... | collective-permute-start | bytes 2654216 | tf_op jit(solution)/shard_map/ppermute | solution.py:19
  84.7 118.5 %collective-permute-start.5 = (bf16[288,1536]{1,0:T(8,128)(2,1)}, bf16[288,1536]{1,0:T(8,128)(2,1)}, u32[]{:S(2)}, u32[]{:S(2)}) collective-permute-start(bf16[288,1536]{1,0:T(8,128)(2,1)} %collective-permute-done.3), channel_id=1, source_target_pairs={{0,13},{1,0},{4,1},{5,4},{8,5},{9,8},{12,9},{13,12},{2,15},{3,2},{... | collective-permute-start | bytes 2654216 | tf_op jit(solution)/shard_map/ppermute | solution.py:24
  110.0 107.4 %collective-permute-start.6 = (bf16[288,1536]{1,0:T(8,128)(2,1)S(1)}, bf16[288,1536]{1,0:T(8,128)(2,1)}, u32[]{:S(2)}, u32[]{:S(2)}) collective-permute-start(bf16[288,1536]{1,0:T(8,128)(2,1)S(1)} %collective-permute-done.4), channel_id=1, source_target_pairs={{0,1},{1,4},{4,5},{5,8},{8,9},{9,12},{12,13},{13,0},{2,3},{3,6},{6... | collective-permute-start | bytes 2654216 | tf_op jit(solution)/shard_map/ppermute | solution.py:19
  269.2 57.4 %copy-start.5 = (bf16[288,1536]{1,0:T(8,128)(2,1)S(1)}, bf16[288,1536]{1,0:T(8,128)(2,1)}, u32[]{:S(2)}) copy-start(bf16[288,1536]{1,0:T(8,128)(2,1)} %param.9) | copy-start | bytes 2654212
  269.2 57.4 %copy-start.6 = (f32[1536]{0:T(1024)S(1)}, f32[1536]{0:T(1024)}, u32[]{:S(2)}) copy-start(f32[1536]{0:T(1024)} %param.11) | copy-start | bytes 18436
  326.6 8.1 %copy-start.1 = (bf16[288,1536]{1,0:T(8,128)(2,1)S(1)}, bf16[288,1536]{1,0:T(8,128)(2,1)}, u32[]{:S(2)}) copy-start(bf16[288,1536]{1,0:T(8,128)(2,1)} %param.6) | copy-start | bytes 2654212
Sparse Core Ops, SparseCore 0:
  9.0 117.7 all-gather.2
  285.5 41.0 all-gather.4
